TPU v7x, 128 devices: a whole 4x4x4 slice. The times are simulated.
128 devices in a mesh: expert: 2 (over z_lo), tensor: 64 (over z_hi, x, y, core).
Axes of the slice: x: 4, y: 4, z: 4 (z_hi: 2, z_lo: 2; z = z_hi * 2 + z_lo), core: 2. Of those that a mesh axis runs over, the one named last changes fastest.
Arguments:
- tokens: bfloat16 [512, 6144], P(('expert', 'tensor')), may hold values from -6 to 6
- gate_weights: bfloat16 [512, 2], P(('expert', 'tensor')), may hold values from 0.19921875 to 1
- expert_ids: int32 [512, 2], P(('expert', 'tensor')), may hold values from 0 to 3, all different within a row; in each aligned block of 512 rows (0 to 511, 512 to 1023, ...) at most 384 rows name the same one
- w_gate: bfloat16 [4, 6144, 16384], P('expert', None, 'tensor'), may hold values from -0.078125 to 0.078125
- w_up: bfloat16 [4, 6144, 16384], P('expert', None, 'tensor'), may hold values from -0.078125 to 0.078125
- w_down: bfloat16 [4, 16384, 6144], P('expert', 'tensor'), may hold values from -0.046875 to 0.046875
Outputs:
- mixed: bfloat16 [512, 6144], P(('expert', 'tensor'))
Inputs may be any that keep to these rules, and one draw needn't show every extreme that they name: `expert_ids`: the 2 ids of a token differ; every expert is named by at most 384 tokens, a bound that some block reaches.
All inputs are finite; a program needn't handle non-finite values.
Results may differ from a plain program's by a relative error of at most 0.0049.
Values may be sent and summed in bfloat16 or wider, within the bound.
A program may use at most 192 MiB of HBM per device.

v0:
```python
import jax
import jax.numpy as jnp
from jax import lax
from jax.sharding import PartitionSpec as P


def routing_lists(expert_ids, gate_weights, expert, capacity):
    matches = expert_ids == expert
    chosen = jnp.any(matches, axis=1)
    weight = jnp.sum(jnp.where(matches, gate_weights.astype(jnp.float32), jnp.float32(0.0)), axis=1)
    ranking = jnp.cumsum(chosen.astype(jnp.int32)) - 1
    target = jnp.where(chosen, ranking, capacity)
    token_count = expert_ids.shape[0]
    slot_tok = (
        jnp.full((capacity,), token_count, jnp.int32)
        .at[target]
        .set(jnp.arange(token_count, dtype=jnp.int32), mode="drop")
    )
    slot_gate = jnp.zeros((capacity,), jnp.float32).at[target].set(weight, mode="drop")
    slot_count = jnp.sum(chosen.astype(jnp.int32))
    return (slot_tok, slot_gate, slot_count)


def expert_rows(slot_rows, gate_mat, up_mat, down_mat):
    gate_proj = jnp.dot(slot_rows, gate_mat, preferred_element_type=jnp.float32)
    up_proj = jnp.dot(slot_rows, up_mat, preferred_element_type=jnp.float32)
    hidden = (jax.nn.silu(gate_proj) * up_proj).astype(jnp.bfloat16)
    return jnp.dot(hidden, down_mat, preferred_element_type=jnp.float32)


def place_rows(values, positions, first_row, row_count):
    inside = (positions >= first_row) & (positions < first_row + row_count)
    target = jnp.where(inside, positions, row_count)
    table = jnp.zeros((row_count, values.shape[1]), jnp.float32)
    return table.at[target].add(values, mode="drop")


def shards(tokens, gate_weights, expert_ids, w_gate, w_up, w_down):
    all_tokens, all_gates = (
        lax.all_gather(tokens, ("expert", "tensor"), axis=0, tiled=True),
        lax.all_gather(gate_weights, ("expert", "tensor"), axis=0, tiled=True),
    )
    all_ids = lax.all_gather(expert_ids, ("expert", "tensor"), axis=0, tiled=True)
    token_count = all_tokens.shape[0]
    local_count = w_gate.shape[0]
    capacity = 3 * token_count // 4
    group_index = lax.axis_index("expert")
    weighted_list = []
    place_list = []
    for local_expert in range(local_count):
        expert = group_index * local_count + local_expert
        slot_tok, slot_gate, slot_count = routing_lists(all_ids, all_gates, expert, capacity)
        slot_rows = all_tokens[jnp.minimum(slot_tok, token_count - 1)]
        expert_out = expert_rows(
            slot_rows, w_gate[local_expert], w_up[local_expert], w_down[local_expert]
        )
        weighted = expert_out * slot_gate[:, None]
        weighted_list.append(weighted)
        place_list.append(slot_tok)
    values = jnp.concatenate(weighted_list, axis=0)
    places = jnp.concatenate(place_list, axis=0)
    n_tensor = lax.axis_size("tensor")
    n_expert = lax.axis_size("expert")
    tok_dev = token_count // (n_tensor * n_expert)
    summed = lax.psum_scatter(
        place_rows(values, places, jnp.int32(0), tok_dev * lax.axis_size(("expert", "tensor"))),
        ("expert", "tensor"),
        scatter_dimension=0,
        tiled=True,
    )
    return summed.astype(jnp.bfloat16)


def solution(mesh):
    in_specs = (
        P(("expert", "tensor"), None),
        P(("expert", "tensor"), None),
        P(("expert", "tensor"), None),
        P("expert", None, "tensor"),
        P("expert", None, "tensor"),
        P("expert", "tensor", None),
    )
    out_specs = P(("expert", "tensor"), None)
    return jax.shard_map(shards, mesh=mesh, in_specs=in_specs, out_specs=out_specs, check_vma=False)
```

profile of v0, /device:TPU:1, one launch (start us, length us, event | category | flops | bytes accessed | tf_op | source)
XLA Modules:
  0.0 640.6 jit_solution(16866157902335160404)
XLA Ops:
  6.5 0.0 all-gather.5.cloned.1.call-start
  6.5 0.7 all-gather.5.cloned.1.call-update
  7.3 180.7 %all-gather = s32[128,4,2]{1,2,0:T(2,128)S(1)} all-gather(s32[1,4,2]{1,2,0:T(2,128)} %bitcast.48), channel_id=1, replica_groups=mesh['expert'=2,'tensor'=64] {'expert','tensor'}, dimensions={0}, use_global_device_ids=true | all-gather | bytes 4128 | tf_op jit(solution)/shard_map/all_gather | solution.py:43
  188.0 0.4 fusion.49
  188.4 0.1 reduce_or.25
  188.5 0.1 reduce_or.23
  188.6 0.1 reshape.206
  188.7 0.3 reduce-window.24
  189.0 0.1 slice.34
  189.2 0.1 reshape.205
  189.3 0.3 reduce-window.16
  189.6 0.1 slice.32
  189.7 170.8 %all-gather.2 = bf16[128,4,2]{1,2,0:T(2,128)(2,1)S(1)} all-gather(bf16[1,4,2]{1,2,0:T(2,128)(2,1)} %bitcast.49), channel_id=1, replica_groups=mesh['expert'=2,'tensor'=64] {'expert','tensor'}, dimensions={0}, use_global_device_ids=true | all-gather | bytes 2064 | tf_op jit(solution)/shard_map/all_gather | solution.py:41
  360.5 0.4 fusion.47
  360.9 0.1 reshape.284
  361.0 0.1 reshape.285
  361.1 0.1 slice_reduce_fusion
  361.2 0.1 add_add_fusion
  361.3 2.4 scatter_custom_fusion.1
  363.8 0.1 slice_reduce_fusion.1
  363.9 0.1 add_add_fusion.1
  364.0 2.4 scatter_custom_fusion
  366.4 2.4 scatter_custom_fusion.2
  368.8 2.6 scatter_custom_fusion.3
  371.6 0.0 all-gather.5.cloned.1.call-done
  371.6 10.4 %reshape.268 = bf16[512,6144]{1,0:T(8,128)(2,1)} reshape(bf16[128,4,6144]{2,1,0:T(4,128)(2,1)} %all-gather.5.cloned.1.call-done) | data formatting | bytes 12582912
  382.0 15.2 %gather_fusion = bf16[384,6144]{1,0:T(8,128)(2,1)} fusion(bf16[512,6144]{1,0:T(8,128)(2,1)} %reshape.268, s32[1024]{0:T(1024)S(1)} %get-tuple-element.10), kind=kCustom, calls=%fused_computation | custom fusion | bytes 9438720 | tf_op jit(solution)/shard_map/gather | solution.py:53
  397.3 15.7 %gather_fusion.1 = bf16[384,6144]{1,0:T(8,128)(2,1)} fusion(bf16[512,6144]{1,0:T(8,128)(2,1)} %reshape.268, s32[1024]{0:T(1024)S(1)} %get-tuple-element.9), kind=kCustom, calls=%fused_computation.1 | custom fusion | bytes 9438720 | tf_op jit(solution)/shard_map/gather | solution.py:53
  413.0 0.0 copy-start
  413.0 4.8 fusion.10
  417.8 0.0 copy-done
  417.8 3.3 fusion.5
  421.2 13.0 %convolution_multiply_fusion.1 = f32[384,6144]{1,0:T(8,128)} fusion(f32[384]{0:T(512)S(1)} %scatter_custom_fusion.2, bf16[2,256,6144]{2,1,0:T(8,128)(2,1)} %param.11, bf16[384,6144]{1,0:T(8,128)(2,1)} %gather_fusion, bf16[2,6144,256]{2,1,0:T(8,128)(2,1)} %param.10, f32[384,256]{1,0:T(8,128)S(1)} %fusion.10), kind=kOutput, calls=%fused_computation.9 | convolution fusion | flops 2418868224 | bytes 20841984 | tf_op jit(solution)/shard_map/dot_general | solution.py:28
  434.1 12.9 %convolution_multiply_fusion = f32[384,6144]{1,0:T(8,128)} fusion(f32[384]{0:T(512)S(1)} %scatter_custom_fusion.3, bf16[2,256,6144]{2,1,0:T(8,128)(2,1)} %param.11, bf16[384,6144]{1,0:T(8,128)(2,1)} %gather_fusion.1, bf16[2,6144,256]{2,1,0:T(8,128)(2,1)} %param.10, f32[384,256]{1,0:T(8,128)S(1)} %fusion.5), kind=kOutput, calls=%fused_computation.8 | convolution fusion | flops 2418868224 | bytes 20841984 | tf_op jit(solution)/shard_map/dot_general | solution.py:28
  447.0 14.3 %pad_maximum_fusion = f32[768,6144]{1,0:T(8,128)} fusion(f32[384,6144]{1,0:T(8,128)} %convolution_multiply_fusion, f32[384,6144]{1,0:T(8,128)} %convolution_multiply_fusion.1), kind=kLoop, calls=%fused_computation.7 | loop fusion | flops 4718592 | bytes 37748736 | tf_op jit(solution)/shard_map/concatenate | solution.py:60
  461.3 44.4 %scatter_custom_fusion.4 = f32[512,6144]{1,0:T(8,128)} fusion(s32[768]{0:T(1024)S(1)} %fusion.50, f32[768,6144]{1,0:T(8,128)} %pad_maximum_fusion, f32[]{:T(128)} %constant.12.clone.1), kind=kCustom, calls=%fused_computation.10 | custom fusion | flops 4718592 | bytes 12583424 | tf_op jit(solution)/shard_map/scatter-add | solution.py:35
  505.7 126.3 %all-reduce.2 = bf16[512,6144]{1,0:T(8,128)(2,1)} all-reduce(f32[512,6144]{1,0:T(8,128)} %scatter_custom_fusion.4), channel_id=2, replica_groups=mesh['expert'=2,'tensor'=64] {'expert','tensor'}, use_global_device_ids=true, to_apply=%region_13.14.clone | all-reduce | flops 3145728 | bytes 18874368
  632.0 1.5 dynamic-slice_convert_fusion
  (14 shorter events, 0.2 us)
Async XLA Ops:
  6.5 365.1 %all-gather.5.cloned.1.call-start = ((), (), s32[]{:S(2)}) async-start(), calls=%async_computation | async-start | bytes 6340608 | tf_op jit(solution)/shard_map/all_gather | solution.py:40
  413.0 4.9 copy-start
Sparse Core Ops, SparseCore 0:
  9.1 202.6 all-gather.4
where the time goes:
time: 648 us; the launch traced here: 641 us
  blocking collectives  478 us (74%)
  other arithmetic  60.4 us (9%)
  local copies, waits for them, and re-layouts  53.9 us (8%)
  matrix products  34 us (5%)
  between operations  13.8 us (2%)
    all_gather x1, blocking collectives, shards(): lax.all_gather(expert_ids, ('expert', 'tensor'), axis=0, tiled=True)  181 us
    all_gather x1, blocking collectives, shards(): lax.all_gather(gate_weights, ('expert', 'tensor'), axis=0, tiled=True)  171 us
    unnamed x1, blocking collectives  126 us
    scatter-add x1, other arithmetic, place_rows(): return table.at[target].add(values, mode='drop')  44.4 us
    gather x2, local copies, waits for them, and re-layouts, shards(): slot_rows = all_tokens[jnp.minimum(slot_tok, token_count - 1)]  30.9 us
    dot_general x2, matrix products, expert_rows(): return jnp.dot(hidden, down_mat, preferred_element_type=jnp.float32)  25.9 us
    concatenate x1, other arithmetic, shards(): values = jnp.concatenate(weighted_list, axis=0)  14.3 us
  transfers between devices with their start and end apart: 1, of which 0 were waited for; matrix products, arithmetic and copies ran while one was open for 2% of the time, Pallas kernels for 0%

commit v1 on v0

v1 whole, which is shorter than its diff:
```python
import functools

import jax
import jax.numpy as jnp
from jax import lax
from jax.experimental import pallas as pl
from jax.experimental.pallas import tpu as pltpu
from jax.sharding import PartitionSpec as P

MESH = pl.DeviceIdType.MESH
BF = jnp.bfloat16
F32 = jnp.float32
ORDER = ((0, 1, 2), (1, 2, 0), (2, 0, 1))
PART = 1024
HALF = 3 * PART
GATE = 128
WIDE = HALF + GATE
START = (0, PART + GATE, 2 * PART + GATE)
CUT = (((0, 640), (640, 512)), ((1152, 512), (1664, 512)), ((2176, 512), (2688, 512)))
WHOLE = ((0, 1152), (1152, 1024), (2176, 1024))


def kernel(tok, ids, gts, wg, wu, wd, out, x_all, st, wgs, wus, wds, xs, acc, hid, own, own16, sp, rp,
           ma, ra, ta, ta16, mb, rb, tb, mc, rc, sd, rd,
           lsem, wsem, s0, r0, ags, agr, fs, fr, ps, pr, rss, rsr, ds, dr):
    e = lax.axis_index("expert")
    t = lax.axis_index("tensor")
    core = lax.rem(t, 2)
    pos = (lax.rem(lax.div(t, 8), 4), lax.rem(lax.div(t, 2), 4), lax.div(t, 32) * 2 + e)
    other = 1 - core

    def device(axis, step):
        at = list(pos)
        at[axis] = lax.rem(at[axis] + step + 4, 4)
        return (lax.rem(at[2], 2), lax.div(at[2], 2) * 32 + at[0] * 8 + at[1] * 2 + core)

    partner = (e, t + 1 - 2 * core)
    right = [device(a, 1) for a in range(3)]
    left = [device(a, -1) for a in range(3)]

    here = (pos[2], pos[1], pos[0], core)
    local = []
    mine = x_all.at[(core, *here)]
    for h, ref in enumerate((mine, st)):
        half = (core, other)[h]
        for i, (src, dst, n) in enumerate(((0, 0, PART), (PART, PART + GATE, 2 * PART))):
            c = pltpu.make_async_copy(
                tok.at[:, pl.ds(pl.multiple_of(half * HALF + src, PART), n)],
                ref.at[:, pl.ds(dst, n)], lsem.at[h, i])
            c.start()
            local.append(c)
    weights = []
    for i, (src, dst) in enumerate(((wg, wgs), (wu, wus), (wd, wds))):
        c = pltpu.make_async_copy(src, dst, wsem.at[i])
        c.start()
        weights.append(c)

    barrier = pltpu.get_barrier_semaphore()
    for d in [partner] + right + left:
        pl.semaphore_signal(barrier, inc=1, device_id=d, device_id_type=MESH)

    lane = lax.broadcasted_iota(jnp.int32, (4, GATE), 1)
    table = jnp.zeros((4, GATE), F32)
    for j in range(2):
        table += jnp.where(ids[:, j:j + 1] == lane, gts[:, j:j + 1].astype(F32), 0.0)
    mine[:, pl.ds(PART, GATE)] = table.astype(BF)
    st[:, pl.ds(PART, GATE)] = table.astype(BF)

    for c in local:
        c.wait()
    pl.semaphore_wait(barrier, 7)

    sent = []

    def send(src, dst, ssem, rsem, dev):
        c = pltpu.make_async_remote_copy(src_ref=src, dst_ref=dst, send_sem=ssem, recv_sem=rsem,
                                         device_id=dev, device_id_type=MESH)
        c.start()
        sent.append(c)
        return c

    c = send(st, x_all.at[(other, *here)], s0, r0, partner)
    c.wait_recv()

    def block(o, s, q, cols):
        at = []
        for axis in (2, 1, 0):
            if axis == ORDER[o][s]:
                at.append(q)
            elif axis in ORDER[o][:s]:
                at.append(slice(None))
            else:
                at.append(pos[axis])
        return x_all.at[(core, *at, slice(None), slice(None), pl.ds(*cols))]

    def near(o, s, step):
        return lax.rem(pos[ORDER[o][s]] + step + 4, 4)

    def gather(o, s, k, ref, dev):
        return send(ref, ref, ags.at[s, o, k], agr.at[s, o, k], dev)

    passed = {}

    def hand(o, j, step):
        ref = block(o, 2, near(o, 2, step), WHOLE[o])
        passed[o, j] = send(ref, ref, fs.at[o, j], fr.at[o, j], partner)

    for s in range(3):
        moves = {}
        for o in range(3):
            a = ORDER[o][s]
            me = near(o, s, 0)
            moves[o, 0] = gather(o, s, 0, block(o, s, me, CUT[o][0]), right[a])
            moves[o, 2] = gather(o, s, 2, block(o, s, me, CUT[o][1]), left[a])
            moves[o, 1] = gather(o, s, 1, block(o, s, me, CUT[o][1]), right[a])
            moves[o, 3] = gather(o, s, 3, block(o, s, me, CUT[o][0]), left[a])
        if s == 2:
            for o in range(3):
                hand(o, 0, 0)
        for o in range(3):
            a = ORDER[o][s]
            moves[o, 0].wait_recv()
            moves[o, 4] = gather(o, s, 4, block(o, s, near(o, s, -1), CUT[o][0]), right[a])
            moves[o, 2].wait_recv()
            moves[o, 5] = gather(o, s, 5, block(o, s, near(o, s, 1), CUT[o][1]), left[a])
        if s < 2:
            for o in range(3):
                for k in (1, 3, 4, 5):
                    moves[o, k].wait_recv()
        else:
            for o in range(3):
                moves[o, 1].wait_recv()
                hand(o, 1, -1)
                moves[o, 3].wait_recv()
                hand(o, 2, 1)
            for o in range(3):
                moves[o, 4].wait_recv()
                moves[o, 5].wait_recv()
                hand(o, 3, 2)

    for c in weights:
        c.wait()
    for turn, h in enumerate((core, other)):
        for o in range(3):
            if turn == 1:
                for j in range(4):
                    passed[o, j].wait_recv()
            for z in range(4):
                xs[pl.ds(z * 128, 128), :] = x_all[
                    h, z, :, :, :, :, pl.ds(START[o], PART)].reshape(128, PART)
            first = turn == 0 and o == 0

            def project(k, _):
                for m, w in ((0, wgs), (1, wus)):
                    r = jnp.dot(xs[...], w[k, h * 3 + o], preferred_element_type=F32)
                    acc[k, m] = r if first else acc[k, m] + r
                return 0

            lax.fori_loop(0, 2, project, 0)

    table = x_all[core, :, :, :, :, :, pl.ds(PART, GATE)].reshape(512, GATE).astype(F32)
    lane = lax.broadcasted_iota(jnp.int32, (512, GATE), 1)
    for k in range(2):
        g = jnp.sum(jnp.where(lane == 2 * e + k, table, 0.0), axis=1, keepdims=True)
        v = acc[k, 0]
        hid[:, k * 256:(k + 1) * 256] = (v / (1.0 + jnp.exp(-v)) * acc[k, 1] * g).astype(BF)

    def down(h, o, n):
        cols = pl.multiple_of(h * HALF + o * PART + n * 256, 256)
        r = jnp.dot(hid[...], wds[:, pl.ds(cols, 256)], preferred_element_type=F32)
        return pl.ds(pl.multiple_of(n * 256, 256), 256), r.reshape(4, 4, 4, 8, 256)

    pair = {}
    for o in range(3):
        def give(n, _):
            at, r = down(other, o, n)
            sp[o, :, :, :, :, at] = r.astype(BF)
            return 0

        lax.fori_loop(0, 4, give, 0)
        pair[o] = send(sp.at[o], rp.at[o], ps.at[o], pr.at[o], partner)

    moves = {}

    def reduce(s, o, k, src, dst, dev):
        moves[s, o, k] = send(src, dst, rss.at[s, o, k], rsr.at[s, o, k], dev)

    LOW, HIGH = pl.ds(0, 512), pl.ds(512, 512)

    def start(s, o, piece, recv):
        a = ORDER[o][2 - s]
        n = lambda step: near(o, 2 - s, step)
        reduce(s, o, 0, piece(o, n(2), LOW), recv.at[o, 0], right[a])
        reduce(s, o, 1, piece(o, n(2), HIGH), recv.at[o, 1], left[a])
        reduce(s, o, 2, piece(o, n(1), HIGH), recv.at[o, 2], right[a])
        reduce(s, o, 3, piece(o, n(-1), LOW), recv.at[o, 3], left[a])

    def merge(s, o, piece, recv, buf):
        a = ORDER[o][2 - s]
        n = lambda step: near(o, 2 - s, step)
        for k, step, cols, dev in ((0, 1, LOW, right[a]), (1, -1, HIGH, left[a])):
            moves[s, o, k].wait_recv()
            buf[o, k] = (piece(o, n(step), cols)[...] + recv[o, k].astype(F32)).astype(buf.dtype)
            reduce(s, o, 4 + k, buf.at[o, k], recv.at[o, 4 + k], dev)

    def final(s, o, piece, recv, put):
        me = near(o, 2 - s, 0)
        for cols, ks in ((LOW, (3, 4)), (HIGH, (2, 5))):
            r = piece(o, me, cols)[...]
            for k in ks:
                moves[s, o, k].wait_recv()
                r = r + recv[o, k].astype(F32)
            put(o, cols, r)

    def at_a(ref):
        def piece(o, q, cols):
            at = [q if axis == ORDER[o][2] else slice(None) for axis in (2, 1, 0)]
            return ref.at[(o, *at, slice(None), cols)]
        return piece

    def at_b(ref):
        def piece(o, q, cols):
            at = [q if axis == ORDER[o][1] else slice(None) for axis in (2, 1, 0) if axis != ORDER[o][2]]
            return ref.at[(o, *at, slice(None), cols)]
        return piece

    def at_c(ref):
        return lambda o, q, cols: ref.at[o, q, :, cols]

    for o in range(3):
        pair[o].wait_recv()

        def keep(n, _):
            at, r = down(core, o, n)
            r = r + rp[o, :, :, :, :, at].astype(F32)
            own[o, :, :, :, :, at] = r
            own16[o, :, :, :, :, at] = r.astype(BF)
            return 0

        lax.fori_loop(0, 4, keep, 0)
        start(0, o, at_a(own16), ra)
    for o in range(3):
        merge(0, o, at_a(own), ra, ma)

    def put_a(o, cols, r):
        ta[o, :, :, :, cols] = r
        ta16[o, :, :, :, cols] = r.astype(BF)

    for o in range(3):
        final(0, o, at_a(own), ra, put_a)
        start(1, o, at_b(ta16), rb)
    for o in range(3):
        merge(1, o, at_b(ta), rb, mb)

    def put_b(o, cols, r):
        tb[o, :, :, cols] = r

    for o in range(3):
        final(1, o, at_b(ta), rb, put_b)
        start(2, o, at_c(tb), rc)
    for o in range(3):
        merge(2, o, at_c(tb), rc, mc)

    def put_c(o, cols, r):
        at = pl.ds(o * PART + cols.start, cols.size)
        sd[:, at] = jnp.where(core == 0, r[4:8], r[0:4])
        to = pl.multiple_of(core * HALF + o * PART + cols.start, 512)
        out[:, pl.ds(to, cols.size)] = jnp.where(core == 0, r[0:4], r[4:8]).astype(BF)

    for o in range(3):
        final(2, o, at_c(tb), rc, put_c)
    c = send(sd, rd, ds, dr, partner)
    c.wait_recv()
    out[:, pl.ds(pl.multiple_of(other * HALF, HALF), HALF)] = rd[...].astype(BF)
    for c in sent:
        c.wait_send()


def shards(tokens, gate_weights, expert_ids, w_gate, w_up, w_down):
    anyspace = pl.BlockSpec(memory_space=pl.ANY)
    vmem = pl.BlockSpec(memory_space=pltpu.VMEM)
    dma = pltpu.SemaphoreType.DMA
    return pl.pallas_call(
        kernel,
        out_shape=jax.ShapeDtypeStruct((4, 2 * HALF), BF),
        in_specs=[anyspace, vmem, vmem, anyspace, anyspace, anyspace],
        out_specs=vmem,
        scratch_shapes=[
            pltpu.VMEM((2, 4, 4, 4, 2, 4, WIDE), BF),
            pltpu.VMEM((4, WIDE), BF),
            pltpu.VMEM((2, 6, PART, 256), BF),
            pltpu.VMEM((2, 6, PART, 256), BF),
            pltpu.VMEM((512, 2 * HALF), BF),
            pltpu.VMEM((512, PART), BF),
            pltpu.VMEM((2, 2, 512, 256), F32),
            pltpu.VMEM((512, 512), BF),
            pltpu.VMEM((3, 4, 4, 4, 8, PART), F32),
            pltpu.VMEM((3, 4, 4, 4, 8, PART), BF),
            pltpu.VMEM((3, 4, 4, 4, 8, PART), BF),
            pltpu.VMEM((3, 4, 4, 4, 8, PART), BF),
            pltpu.VMEM((3, 2, 4, 4, 8, 512), BF),
            pltpu.VMEM((3, 6, 4, 4, 8, 512), BF),
            pltpu.VMEM((3, 4, 4, 8, PART), F32),
            pltpu.VMEM((3, 4, 4, 8, PART), BF),
            pltpu.VMEM((3, 2, 4, 8, 512), BF),
            pltpu.VMEM((3, 6, 4, 8, 512), BF),
            pltpu.VMEM((3, 4, 8, PART), F32),
            pltpu.VMEM((3, 2, 8, 512), F32),
            pltpu.VMEM((3, 6, 8, 512), F32),
            pltpu.VMEM((4, HALF), F32),
            pltpu.VMEM((4, HALF), F32),
            dma((2, 2)), dma((3,)), dma, dma, dma((3, 3, 6)), dma((3, 3, 6)), dma((3, 4)), dma((3, 4)),
            dma((3,)), dma((3,)), dma((3, 3, 6)), dma((3, 3, 6)), dma, dma,
        ],
        compiler_params=pltpu.CompilerParams(
            collective_id=0, has_side_effects=True, vmem_limit_bytes=67043328),
        name="moe",
    )(tokens, expert_ids, gate_weights, w_gate.reshape(2, 6, PART, 256), w_up.reshape(2, 6, PART, 256),
      w_down.reshape(512, 2 * HALF))


def solution(mesh):
    rows = P(("expert", "tensor"), None)
    return jax.shard_map(
        shards, mesh=mesh,
        in_specs=(rows, rows, rows, P("expert", None, "tensor"), P("expert", None, "tensor"),
                  P("expert", "tensor", None)),
        out_specs=rows, check_vma=False)
```

time: 648 us -> 86.2 us (0.13); the launches traced: 641 us -> 86 us
  blocking collectives: 478 us -> 0 us
  Pallas kernels: 0 us -> 81.9 us
  other arithmetic: 60.4 us -> 0 us
  local copies, waits for them, and re-layouts: 53.9 us -> 4.09 us
  matrix products: 34 us -> 0 us
  between operations: 13.8 us -> 0.01 us
    all_gather x2 -> x0, blocking collectives: 351 us -> none  [the longest x1 181 us: shards(): lax.all_gather(expert_ids, ('expert', 'tensor'), axis=0, tiled=True)]
    unnamed x1 -> x0, blocking collectives: 126 us -> none
    pallas_call x0 -> x1, Pallas kernels: none -> 81.9 us  [shards(): pl.pallas_call(kernel, out_shape=jax.ShapeDtypeStruct((4, 2 * HALF), BF),...]
    scatter-add x1 -> x0, other arithmetic: 44.4 us -> none  [place_rows(): return table.at[target].add(values, mode='drop')]
    dot_general x4 -> x0, matrix products: 34 us -> none  [the longest x2 25.9 us: expert_rows(): return jnp.dot(hidden, down_mat, preferred_element_type=jnp.float32)]
    gather x2 -> x0, local copies, waits for them, and re-layouts: 30.9 us -> none  [shards(): slot_rows = all_tokens[jnp.minimum(slot_tok, token_count - 1)]]
    concatenate x1 -> x0, other arithmetic: 14.3 us -> none  [shards(): values = jnp.concatenate(weighted_list, axis=0)]
    scatter x4 -> x0, local copies, waits for them, and re-layouts: 9.92 us -> none  [the longest x2 5.05 us: routing_lists(): jnp.zeros((capacity,), jnp.float32).at[target].set(weight, mode='drop')]
  transfers between devices with their start and end apart: 1 -> 0, of which waited for: 0 -> 0; matrix products, arithmetic and copies ran while one was open for 2% -> 0% of each run, Pallas kernels for 0% -> 0%
where the time goes in v1:
time: 86.2 us; the launch traced here: 86 us
  Pallas kernels  81.9 us (95%)
  local copies, waits for them, and re-layouts  4.09 us (5%)
    pallas_call x1, Pallas kernels, shards(): pl.pallas_call(kernel, out_shape=jax.ShapeDtypeStruct((4, 2 * HALF), BF),...  81.9 us
    unnamed x3, local copies, waits for them, and re-layouts  4.09 us

profile of v1, /device:TPU:1, one launch (start us, length us, event | category | flops | bytes accessed | tf_op | source)
XLA Modules:
  0.0 86.0 jit_solution(8143764071197911672)
XLA Ops:
  0.0 1.3 %copy.8.gts = bf16[4,2]{1,0:T(4,128)(2,1)} copy(bf16[4,2]{0,1:T(2,128)(2,1)} %param.7) | data formatting | bytes 32 | tf_op args[1]
  1.3 1.3 %copy.7.ids = s32[4,2]{1,0:T(4,128)} copy(s32[4,2]{0,1:T(2,128)} %param.8) | data formatting | bytes 64 | tf_op args[2]
  2.7 81.9 %moe.1 = bf16[4,6144]{1,0:T(4,128)(2,1)} custom-call(bf16[4,6144]{1,0:T(4,128)(2,1)} %tok.1, s32[4,2]{1,0:T(4,128)} %copy.7.ids, bf16[4,2]{1,0:T(4,128)(2,1)} %copy.8.gts, bf16[2,6,1024,256]{3,2,1,0:T(8,128)(2,1)} %bitcast.3, bf16[2,6,1024,256]{3,2,1,0:T(8,128)(2,1)} %bitcast.4, bf16[512,6144]{1,0:T(8,128)(2,1)} %bitcast.5), custom_call_target="tpu_custom_call" | custom-call | tf_op jit(solution)/shard_map/moe/pallas_call | solution.py:283
  84.6 1.4 %copy.10 = bf16[4,6144]{1,0:T(4,128)(2,1)} copy(bf16[4,6144]{1,0:T(4,128)(2,1)} %moe.1) | data formatting | bytes 98304

commit v2 on v1

v2 whole, which is shorter than its diff:
```python
import functools

import jax
import jax.numpy as jnp
from jax import lax
from jax.experimental import pallas as pl
from jax.experimental.pallas import tpu as pltpu
from jax.sharding import PartitionSpec as P

MESH = pl.DeviceIdType.MESH
BF = jnp.bfloat16
F32 = jnp.float32
ORDER = ((0, 1, 2), (1, 2, 0), (2, 0, 1))
PART = 1024
HALF = 3 * PART
GATE = 128
WIDE = HALF + GATE
STEPS = (1, -1, 2)
START = (0, PART + GATE, 2 * PART + GATE)
CUT = (((0, 640), (640, 512)), ((1152, 512), (1664, 512)), ((2176, 512), (2688, 512)))
WHOLE = ((0, 1152), (1152, 1024), (2176, 1024))


def kernel(tok, ids, gts, wg, wu, wd, out, x_all, st, idv, gtv, wgs, wus, wds, xs, acc, hid, own, own16,
           sp, rp, ma, ra, ta, tb16, rb, tb, rc, sd, rd,
           lsem, wsem, s0, r0, a1s, a1r, a2s, a2r, a3s, a3r, fs, fr, ps, pr, b1s, b1r, b2s, b2r, b3s, b3r,
           ds, dr):
    e = lax.axis_index("expert")
    t = lax.axis_index("tensor")
    core = lax.rem(t, 2)
    pos = (lax.rem(lax.div(t, 8), 4), lax.rem(lax.div(t, 2), 4), lax.div(t, 32) * 2 + e)
    other = 1 - core

    def near(axis, step):
        return lax.rem(pos[axis] + step + 4, 4)

    def device(axis, step):
        at = list(pos)
        at[axis] = near(axis, step)
        return (lax.rem(at[2], 2), lax.div(at[2], 2) * 32 + at[0] * 8 + at[1] * 2 + core)

    partner = (e, t + 1 - 2 * core)
    peers = [[device(a, step) for step in STEPS] for a in range(3)]

    barrier = pltpu.get_barrier_semaphore()
    for d in [partner] + peers[0] + peers[1] + peers[2]:
        pl.semaphore_signal(barrier, inc=1, device_id=d, device_id_type=MESH)

    here = (pos[2], pos[1], pos[0], core)
    mine = x_all.at[(core, *here)]
    local = []

    def load(src, dst, sem):
        c = pltpu.make_async_copy(src, dst, sem)
        c.start()
        return c

    local.append(load(ids, idv, lsem.at[2, 0]))
    local.append(load(gts, gtv, lsem.at[2, 1]))
    for h, ref in enumerate((mine, st)):
        half = (core, other)[h]
        for i, (src, dst, n) in enumerate(((0, 0, PART), (PART, PART + GATE, 2 * PART))):
            local.append(load(tok.at[:, pl.ds(pl.multiple_of(half * HALF + src, PART), n)],
                              ref.at[:, pl.ds(dst, n)], lsem.at[h, i]))
    weights = [load(src, dst, wsem.at[i]) for i, (src, dst) in enumerate(((wg, wgs), (wu, wus), (wd, wds)))]

    local[0].wait()
    local[1].wait()
    lane = lax.broadcasted_iota(jnp.int32, (4, GATE), 1)
    row = lax.broadcasted_iota(jnp.int32, (4, GATE), 0)
    table = jnp.zeros((4, GATE), F32)
    gvals = gtv[...].astype(F32)
    for j in range(2):
        for r in range(4):
            hit = (row == r) & (lane == idv[j:j + 1, r:r + 1])
            table += jnp.where(hit, gvals[j:j + 1, r:r + 1], 0.0)
    mine[:, pl.ds(PART, GATE)] = table.astype(BF)
    st[:, pl.ds(PART, GATE)] = table.astype(BF)

    for c in local[2:]:
        c.wait()
    pl.semaphore_wait(barrier, 10)

    sent = []

    def send(src, dst, ssem, rsem, dev):
        c = pltpu.make_async_remote_copy(src_ref=src, dst_ref=dst, send_sem=ssem, recv_sem=rsem,
                                         device_id=dev, device_id_type=MESH)
        c.start()
        sent.append(c)
        return c

    c = send(st, x_all.at[(other, *here)], s0, r0, partner)
    acc[...] = jnp.zeros_like(acc)
    c.wait_recv()
    every = slice(None)

    def spot(o, q3, q2, q1=every):
        at = dict(zip(ORDER[o], (q1, q2, q3)))
        return (at[2], at[1], at[0])

    def block(o, q3, q2, q1, cols):
        return x_all.at[(core, *spot(o, q3, q2, q1), every, every, pl.ds(*cols))]

    first, second, third = {}, {}, {}
    for o in range(3):
        a1, a2, a3 = ORDER[o]
        ref = block(o, pos[a3], pos[a2], pos[a1], WHOLE[o])
        for i in range(3):
            first[o, i] = send(ref, ref, a1s.at[o, i], a1r.at[o, i], peers[a1][i])

    def direct(o, j):
        a1, a2, a3 = ORDER[o]
        q2 = near(a2, (0, -1, 1, 2)[j])
        for k, to, cut in ((0, 0, 0), (2, 1, 1), (1, 0, 1), (3, 1, 0)):
            ref = block(o, pos[a3], q2, every, CUT[o][cut])
            third[o, j, k] = send(ref, ref, a3s.at[o, j, k], a3r.at[o, j, k], peers[a3][to])

    def relay(o, j):
        a1, a2, a3 = ORDER[o]
        q2 = near(a2, (0, -1, 1, 2)[j])
        for k, to, cut in ((0, 0, 0), (2, 1, 1)):
            third[o, j, k].wait_recv()
            ref = block(o, near(a3, (-1, 1)[to]), q2, every, CUT[o][cut])
            third[o, j, 4 + to] = send(ref, ref, a3s.at[o, j, 4 + to], a3r.at[o, j, 4 + to], peers[a3][to])

    passed = {}

    def hand(o, j, step):
        ref = block(o, near(ORDER[o][2], step), every, every, WHOLE[o])
        passed[o, j] = send(ref, ref, fs.at[o, j], fr.at[o, j], partner)

    def project(h, o, steps):
        n = len(steps) * 128
        for i, step in enumerate(steps):
            xs[i * 128:(i + 1) * 128, :] = x_all[
                (h, *spot(o, near(ORDER[o][2], step), every), every, every, pl.ds(START[o], PART))
            ].reshape(128, PART)

        def one(k, _):
            for m, w in ((0, wgs), (1, wus)):
                r = jnp.dot(xs[0:n, :], w[k, h * 3 + o], preferred_element_type=F32)
                for i, step in enumerate(steps):
                    at = (k, m, *spot(o, near(ORDER[o][2], step), every))
                    acc[at] = acc[at] + r[i * 128:(i + 1) * 128].reshape(4, 4, 8, 256)
            return 0

        lax.fori_loop(0, 2, one, 0)

    for o in range(3):
        a1, a2, a3 = ORDER[o]
        for i in range(3):
            first[o, i].wait_recv()
        ref = block(o, pos[a3], pos[a2], every, WHOLE[o])
        for i in range(3):
            second[o, i] = send(ref, ref, a2s.at[o, i], a2r.at[o, i], peers[a2][i])
        direct(o, 0)
    for i in range(3):
        for o in range(3):
            second[o, i].wait_recv()
            direct(o, i + 1)
            if i == 2:
                hand(o, 0, 0)
    for o in range(3):
        relay(o, 0)
    weights[0].wait()
    weights[1].wait()
    for j in range(3):
        project(core, j, (0,))
        for o in range(3):
            relay(o, j + 1)
    for o in range(3):
        for j in range(4):
            third[o, j, 1].wait_recv()
            third[o, j, 3].wait_recv()
        hand(o, 1, -1)
        hand(o, 2, 1)
    for o in range(3):
        project(core, o, (-1, 1))
    for o in range(3):
        for j in range(4):
            third[o, j, 4].wait_recv()
            third[o, j, 5].wait_recv()
        hand(o, 3, 2)
    for o in range(3):
        project(core, o, (2,))
    for o in range(3):
        for j in range(4):
            passed[o, j].wait_recv()
        project(other, o, (0, 1, -1, 2))

    table = x_all[core, :, :, :, :, :, pl.ds(PART, GATE)].reshape(512, GATE).astype(F32)
    lane = lax.broadcasted_iota(jnp.int32, (512, GATE), 1)
    for k in range(2):
        g = jnp.sum(jnp.where(lane == 2 * e + k, table, 0.0), axis=1, keepdims=True)
        v = acc[k, 0].reshape(512, 256)
        u = acc[k, 1].reshape(512, 256)
        hid[:, k * 256:(k + 1) * 256] = (v / (1.0 + jnp.exp(-v)) * u * g).astype(BF)

    weights[2].wait()

    def down(h, o, n):
        cols = pl.multiple_of(h * HALF + o * PART + n * 256, 256)
        r = jnp.dot(hid[...], wds[:, pl.ds(cols, 256)], preferred_element_type=F32)
        return pl.ds(pl.multiple_of(n * 256, 256), 256), r.reshape(4, 4, 4, 8, 256)

    LOW, HIGH = pl.ds(0, 512), pl.ds(512, 512)
    pair = {}
    for o in range(3):
        def give(n, _):
            at, r = down(other, o, n)
            sp[o, :, :, :, :, at] = r.astype(BF)
            return 0

        for u, cols in enumerate((LOW, HIGH)):
            lax.fori_loop(2 * u, 2 * u + 2, give, 0)
            at = (o, every, every, every, every, cols)
            pair[o, u] = send(sp.at[at], rp.at[at], ps.at[o, u], pr.at[o, u], partner)

    AWAY = (2, 1, -1, 0)
    moves = {}

    def begin(o):
        a1, a2, a3 = ORDER[o]
        for ks in (((0, 2, LOW, 0), (1, 2, HIGH, 1)), ((2, 1, HIGH, 0), (3, -1, LOW, 1))):
            for j in range(4):
                for k, step, cols, to in ks:
                    src = own16.at[(o, *spot(o, near(a3, step), near(a2, AWAY[j])), every, cols)]
                    moves[o, j, k] = send(src, ra.at[o, j, k], b1s.at[o, j, k], b1r.at[o, j, k], peers[a3][to])

    def merge(o, j):
        a1, a2, a3 = ORDER[o]
        for k, step, cols, to in ((0, 1, LOW, 0), (1, -1, HIGH, 1)):
            moves[o, j, k].wait_recv()
            at = (o, *spot(o, near(a3, step), near(a2, AWAY[j])), every, cols)
            ma[o, j, k] = (own[at] + ra[o, j, k].astype(F32)).astype(BF)
            moves[o, j, 4 + k] = send(ma.at[o, j, k], ra.at[o, j, 4 + k], b1s.at[o, j, 4 + k],
                                      b1r.at[o, j, 4 + k], peers[a3][to])

    turn = {}

    def final(o, j):
        a1, a2, a3 = ORDER[o]
        for cols, ks in ((LOW, (3, 4)), (HIGH, (2, 5))):
            r = own[(o, *spot(o, pos[a3], near(a2, AWAY[j])), every, cols)]
            for k in ks:
                moves[o, j, k].wait_recv()
                r = r + ra[o, j, k].astype(F32)
            if j < 3:
                tb16[o, j, :, :, cols] = r.astype(BF)
            else:
                ta[o, :, :, cols] = r
        if j < 3:
            turn[o, j] = send(tb16.at[o, j], rb.at[o, j], b2s.at[o, j], b2r.at[o, j], peers[a2][(2, 0, 1)[j]])

    for o in range(3):
        def keep(n, _):
            at, r = down(core, o, n)
            r = r + rp[o, :, :, :, :, at].astype(F32)
            own[o, :, :, :, :, at] = r
            own16[o, :, :, :, :, at] = r.astype(BF)
            return 0

        for u in range(2):
            pair[o, u].wait_recv()
            lax.fori_loop(2 * u, 2 * u + 2, keep, 0)
        begin(o)
    for j in range(4):
        for o in range(3):
            merge(o, j)
            if j > 0:
                final(o, j - 1)
    last = {}
    for o in range(3):
        final(o, 3)
    for o in range(3):
        a1, a2, a3 = ORDER[o]
        r = ta[o]
        for j in range(3):
            turn[o, j].wait_recv()
            r = r + rb[o, j].astype(F32)
        tb[o] = r
        for i in range(3):
            last[o, i] = send(tb.at[o, near(a1, STEPS[i])], rc.at[o, i], b3s.at[o, i], b3r.at[o, i], peers[a1][i])
    for o in range(3):
        r = tb[o, pos[ORDER[o][0]]]
        for i in range(3):
            last[o, i].wait_recv()
            r = r + rc[o, i]
        sd[:, pl.ds(o * PART, PART)] = jnp.where(core == 0, r[4:8], r[0:4])
        to = pl.multiple_of(core * HALF + o * PART, PART)
        out[:, pl.ds(to, PART)] = jnp.where(core == 0, r[0:4], r[4:8]).astype(BF)
    c = send(sd, rd, ds, dr, partner)
    c.wait_recv()
    out[:, pl.ds(pl.multiple_of(other * HALF, HALF), HALF)] = rd[...].astype(BF)
    for c in sent:
        c.wait_send()


def shards(tokens, gate_weights, expert_ids, w_gate, w_up, w_down):
    anyspace = pl.BlockSpec(memory_space=pl.ANY)
    vmem = pl.BlockSpec(memory_space=pltpu.VMEM)
    dma = pltpu.SemaphoreType.DMA
    return pl.pallas_call(
        kernel,
        out_shape=jax.ShapeDtypeStruct((4, 2 * HALF), BF),
        in_specs=[anyspace] * 6,
        out_specs=vmem,
        scratch_shapes=[
            pltpu.VMEM((2, 4, 4, 4, 2, 4, WIDE), BF),
            pltpu.VMEM((4, WIDE), BF),
            pltpu.VMEM((2, 4), jnp.int32),
            pltpu.VMEM((2, 4), BF),
            pltpu.VMEM((2, 6, PART, 256), BF),
            pltpu.VMEM((2, 6, PART, 256), BF),
            pltpu.VMEM((512, 2 * HALF), BF),
            pltpu.VMEM((512, PART), BF),
            pltpu.VMEM((2, 2, 4, 4, 4, 8, 256), F32),
            pltpu.VMEM((512, 512), BF),
            pltpu.VMEM((3, 4, 4, 4, 8, PART), F32),
            pltpu.VMEM((3, 4, 4, 4, 8, PART), BF),
            pltpu.VMEM((3, 4, 4, 4, 8, PART), BF),
            pltpu.VMEM((3, 4, 4, 4, 8, PART), BF),
            pltpu.VMEM((3, 4, 2, 4, 8, 512), BF),
            pltpu.VMEM((3, 4, 6, 4, 8, 512), BF),
            pltpu.VMEM((3, 4, 8, PART), F32),
            pltpu.VMEM((3, 3, 4, 8, PART), BF),
            pltpu.VMEM((3, 3, 4, 8, PART), BF),
            pltpu.VMEM((3, 4, 8, PART), F32),
            pltpu.VMEM((3, 3, 8, PART), F32),
            pltpu.VMEM((4, HALF), F32),
            pltpu.VMEM((4, HALF), F32),
            dma((3, 2)), dma((3,)), dma, dma, dma((3, 3)), dma((3, 3)), dma((3, 3)), dma((3, 3)),
            dma((3, 4, 6)), dma((3, 4, 6)), dma((3, 4)), dma((3, 4)), dma((3, 2)), dma((3, 2)),
            dma((3, 4, 6)), dma((3, 4, 6)), dma((3, 3)), dma((3, 3)), dma((3, 3)), dma((3, 3)), dma, dma,
        ],
        compiler_params=pltpu.CompilerParams(
            collective_id=0, has_side_effects=True, vmem_limit_bytes=67043328),
        name="moe",
    )(tokens, expert_ids.T, gate_weights.T, w_gate.reshape(2, 6, PART, 256), w_up.reshape(2, 6, PART, 256),
      w_down.reshape(512, 2 * HALF))


def solution(mesh):
    rows = P(("expert", "tensor"), None)
    return jax.shard_map(
        shards, mesh=mesh,
        in_specs=(rows, rows, rows, P("expert", None, "tensor"), P("expert", None, "tensor"),
                  P("expert", "tensor", None)),
        out_specs=rows, check_vma=False)
```

time: 86.2 us -> 74.4 us (0.86)
  Pallas kernels: 81.9 us -> 72.8 us
  local copies, waits for them, and re-layouts: 4.09 us -> 1.44 us
    pallas_call x1, Pallas kernels: 81.9 us -> 72.8 us  [shards(): pl.pallas_call(kernel, out_shape=jax.ShapeDtypeStruct((4, 2 * HALF), BF),...]
    unnamed x3 -> x1, local copies, waits for them, and re-layouts: 4.09 us -> 1.44 us
where the time goes in v2:
time: 74.4 us; the launch traced here: 74.3 us
  Pallas kernels  72.8 us (98%)
  local copies, waits for them, and re-layouts  1.44 us (2%)
    pallas_call x1, Pallas kernels, shards(): pl.pallas_call(kernel, out_shape=jax.ShapeDtypeStruct((4, 2 * HALF), BF),...  72.8 us

profile of v2, /device:TPU:1, one launch (start us, length us, event | category | flops | bytes accessed | tf_op | source)
XLA Modules:
  0.0 74.3 jit_solution(5374464376667551976)
XLA Ops:
  0.0 72.8 %moe.1 = bf16[4,6144]{1,0:T(4,128)(2,1)} custom-call(bf16[4,6144]{1,0:T(4,128)(2,1)} %tok.1, s32[2,4]{1,0:T(2,128)} %bitcast.8, bf16[2,4]{1,0:T(2,128)(2,1)} %bitcast.9, bf16[2,6,1024,256]{3,2,1,0:T(8,128)(2,1)} %bitcast.5, bf16[2,6,1024,256]{3,2,1,0:T(8,128)(2,1)} %bitcast.6, bf16[512,6144]{1,0:T(8,128)(2,1)} %bitcast.7), custom_call_target="tpu_custom_call" | custom-call | tf_op jit(solution)/shard_map/moe/pallas_call | solution.py:304
  72.9 1.4 %copy.8 = bf16[4,6144]{1,0:T(4,128)(2,1)} copy(bf16[4,6144]{1,0:T(4,128)(2,1)} %moe.1) | data formatting | bytes 98304
